TPU v7x, 256 devices: a whole 4x4x8 slice. The times are simulated.
256 devices in a mesh: slab: 32 (over z, y), snap: 8 (over x, core).
Axes of the slice: x: 4, y: 4, z: 8, core: 2. Of those that a mesh axis runs over, the one named last changes fastest.
Arguments:
- flow: bfloat16 [128, 3, 64, 64, 128], P('snap', None, 'slab'), may hold values from -127 to 127
- large_scale: bfloat16 [3, 64, 64, 128], P(None, 'slab'), may hold values from -6 to 6
- modulation: float32 [128, 64], replicated, may hold values from -15 to 15
- metric: float32 [4, 64, 64, 128], P(None, 'slab'), may hold values from -0.5 to 9.6
Outputs:
- whitened: float32 [128, 3, 64, 64, 128], P(None, None, 'slab', 'snap')
All inputs are finite; a program needn't handle non-finite values.
Results may differ from a plain program's by a relative error of at most 0.0003.
Values may be sent and summed in bfloat16 or wider, within the bound.
A program may use at most 64 MiB of HBM per device.

v0:
```python
import jax
import jax.numpy as jnp
from jax import lax
from jax.sharding import PartitionSpec as P

NSITER = 6


def with_halo(block, sides, width):
    for axis, dim in sides:
        count = lax.axis_size(axis)
        forward = [(i, i + 1) for i in range(count - 1)]
        backward = [(target, source) for source, target in forward]
        low = lax.ppermute(
            lax.slice_in_dim(block, block.shape[dim] - width, None, axis=dim), axis, forward
        )
        high = lax.ppermute(lax.slice_in_dim(block, 0, width, axis=dim), axis, backward)
        block = jnp.concatenate([low, block, high], axis=dim)
    return block


def vorticity(velocity, metric):
    metric_x = metric[0]
    shear_xy = metric[1]
    metric_y = metric[2]
    metric_z = metric[3]

    def along_x(values):
        return 0.5 * (values[..., 1:-1, 2:, :] - values[..., 1:-1, :-2, :])

    def along_y(values):
        return 0.5 * (values[..., 2:, 1:-1, :] - values[..., :-2, 1:-1, :])

    def along_z(values):
        center = values[..., 1:-1, 1:-1, :]
        return 0.5 * (jnp.roll(center, -1, -1) - jnp.roll(center, 1, -1))

    def slope_x(values):
        return metric_x * along_x(values) + shear_xy * along_y(values)

    def slope_y(values):
        return metric_y * along_y(values)

    def slope_z(values):
        return metric_z * along_z(values)

    stream = velocity[..., 0, :, :, :]
    normal = velocity[..., 1, :, :, :]
    spanwise = velocity[..., 2, :, :, :]
    around_x = slope_y(spanwise) - slope_z(normal)
    around_y = slope_z(stream) - slope_x(spanwise)
    around_z = slope_x(normal) - slope_y(stream)
    return jnp.stack([around_x, around_y, around_z], axis=-4)


def wrap_columns(values):
    return jnp.concatenate([values[..., -1:, :], values, values[..., :1, :]], axis=-2)


def whitening(correlation):
    identity = jnp.eye(correlation.shape[0], dtype=correlation.dtype)
    frob_scale = jnp.sqrt(jnp.sum(correlation * correlation) + 1e-06)
    approx = correlation / frob_scale
    inverse = identity
    for repeat in range(NSITER):
        factor = 0.5 * (3.0 * identity - jnp.dot(inverse, approx, precision=lax.Precision.HIGHEST))
        approx = jnp.dot(approx, factor, precision=lax.Precision.HIGHEST)
        inverse = jnp.dot(factor, inverse, precision=lax.Precision.HIGHEST)
    return inverse / jnp.sqrt(frob_scale)


def inner_rows(left_rows, right_rows):
    return lax.dot_general(
        left_rows,
        right_rows,
        (((1,), (1,)), ((), ())),
        precision=lax.Precision.HIGHEST,
        preferred_element_type=jnp.float32,
    )


def planes_padded(flow, large_scale):
    joined = jnp.concatenate([flow, large_scale[None]], axis=0)
    return with_halo(joined, (("slab", 2),), 1)


def per_device(flow, large_scale, modulation, metric):
    snap_count = lax.axis_size("snap")
    slab_count = lax.axis_size("slab")
    own_snaps = flow.shape[0]
    block_cols = flow.shape[3] // snap_count
    snap_index = lax.axis_index("snap")
    mod_ext = jnp.concatenate([modulation[:, -1:], modulation, modulation[:, :1]], axis=1)
    padded = planes_padded(flow, large_scale)
    large_ext = wrap_columns(padded[own_snaps].astype(jnp.float32))
    mod_mine = lax.dynamic_slice_in_dim(mod_ext, snap_index * own_snaps, own_snaps, 0)
    velocity = (
        wrap_columns(padded[:own_snaps].astype(jnp.float32))
        + mod_mine[:, None, None, :, None] * large_ext[None]
    )
    local_fields = vorticity(velocity, metric)
    pieces = local_fields.reshape(
        own_snaps, 3, local_fields.shape[2], snap_count, block_cols, local_fields.shape[4]
    )
    fields = lax.all_to_all(pieces, "snap", split_axis=3, concat_axis=0, tiled=True)[:, :, :, 0]
    snapshot_rows = fields.reshape(fields.shape[0], -1)
    gram_local = inner_rows(snapshot_rows, snapshot_rows)
    gram_total = lax.psum(gram_local, ("slab", "snap"))
    correlation = gram_total / (snapshot_rows.shape[1] * slab_count * snap_count)
    weights = whitening(correlation)
    result = jnp.dot(weights, snapshot_rows, precision=lax.Precision.HIGHEST)
    return result.reshape(fields.shape)


def solution(mesh):
    return jax.shard_map(
        per_device,
        mesh=mesh,
        in_specs=(
            P("snap", None, "slab", None, None),
            P(None, "slab", None, None),
            P(),
            P(None, "slab", None, None),
        ),
        out_specs=P(None, None, "slab", "snap", None),
        check_vma=False,
    )
```

profile of v0, /device:TPU:1, one launch (start us, length us, event | category | flops | bytes accessed | tf_op | source)
XLA Modules:
  0.0 358.1 jit_solution(2387422955889473556)
XLA Ops:
  6.5 2.9 fusion.21
  9.4 4.1 %collective-permute-start = (bf16[17,3,1,64,128]{4,3,2,1,0:T(8,128)(2,1)}, bf16[17,3,1,64,128]{4,3,2,1,0:T(8,128)(2,1)S(1)}, u32[]{:S(2)}, u32[]{:S(2)}) collective-permute-start(bf16[17,3,1,64,128]{4,3,2,1,0:T(8,128)(2,1)} %get-tuple-element.20), channel_id=1, source_target_pairs={{0,8},{8,16},{16,24},{24,32},{32,40},{40,48},{48,56},{56,64},{64,7... | collective-permute-start | bytes 2506760 | tf_op jit(solution)/shard_map/ppermute | solution.py:14
  13.5 1.3 collective-permute-start.1
  15.0 1.0 multiply_bitcast_fusion.2
  15.9 15.1 %collective-permute-done = bf16[17,3,1,64,128]{4,3,2,1,0:T(8,128)(2,1)S(1)} collective-permute-done((bf16[17,3,1,64,128]{4,3,2,1,0:T(8,128)(2,1)}, bf16[17,3,1,64,128]{4,3,2,1,0:T(8,128)(2,1)S(1)}, u32[]{:S(2)}, u32[]{:S(2)}) %collective-permute-start) | collective-permute-done | bytes 835616 | tf_op jit(solution)/shard_map/ppermute | solution.py:14
  31.0 3.8 %collective-permute-done.1 = bf16[17,3,1,64,128]{4,3,2,1,0:T(8,128)(2,1)S(1)} collective-permute-done((bf16[17,3,1,64,128]{4,3,2,1,0:T(8,128)(2,1)}, bf16[17,3,1,64,128]{4,3,2,1,0:T(8,128)(2,1)S(1)}, u32[]{:S(2)}, u32[]{:S(2)}) %collective-permute-start.1) | collective-permute-done | bytes 835616 | tf_op jit(solution)/shard_map/ppermute | solution.py:17
  34.8 0.5 pad_maximum_fusion
  35.3 0.7 slice_convert_fusion
  36.3 1.5 maximum_add_fusion
  37.7 0.5 slice_bitcast_fusion.2
  38.2 0.9 fusion.28
  39.1 0.9 fusion.29
  40.0 0.8 fusion.9
  40.7 1.5 fusion.19
  42.8 43.4 %all_to_all.15 = f32[16,3,2,8,8,128]{5,4,2,1,0,3:T(8,128)} all-to-all(f32[16,3,2,8,8,128]{5,4,2,1,0,3:T(8,128)S(1)} %copy.19), channel_id=1, replica_groups=mesh['slab'=32,'snap'=8] {'snap'}, dimensions={3} | all-to-all | bytes 6291456 | tf_op jit(solution)/shard_map/all_to_all | solution.py:105
  86.2 2.8 reshape_squeeze.3
  89.0 3.2 fusion.34
  92.2 2.4 copy.16
  94.6 242.7 %all-reduce.2.cloned.1.call-done = f32[128,128]{1,0:T(8,128)} async-done(((f32[128,128]{1,0:T(8,128)}), f32[128,128]{1,0:T(8,128)}) %all-reduce.2.cloned.1.call-update) | async-done | bytes 65552 | tf_op jit(solution)/shard_map/psum | solution.py:108
  337.3 1.5 multiply_reduce_fusion
  339.5 1.0 fusion.6
  340.7 1.0 fusion.24
  344.7 3.0 fusion.43
  347.8 3.5 copy.17
  (34 shorter events, 4.0 us)
Async XLA Ops:
  6.5 28.2 %copy-start = (bf16[16,3,2,64,128]{4,3,2,1,0:T(8,128)(2,1)S(1)}, bf16[16,3,2,64,128]{4,3,2,1,0:T(8,128)(2,1)}, u32[]{:S(2)}) copy-start(bf16[16,3,2,64,128]{4,3,2,1,0:T(8,128)(2,1)} %param.4) | copy-start | bytes 4718596
  6.5 28.2 %copy-start.2 = (bf16[3,2,64,128]{3,2,1,0:T(8,128)(2,1)S(1)}, bf16[3,2,64,128]{3,2,1,0:T(8,128)(2,1)}, u32[]{:S(2)}) copy-start(bf16[3,2,64,128]{3,2,1,0:T(8,128)(2,1)} %param.5) | copy-start | bytes 294916
  6.5 8.2 %copy-start.3 = (f32[128,64]{0,1:T(8,128)S(1)}, f32[128,64]{0,1:T(8,128)}, u32[]{:S(2)}) copy-start(f32[128,64]{0,1:T(8,128)} %param.6) | copy-start | bytes 98308
  6.5 330.8 %all-reduce.2.cloned.1.call-start = ((), (), s32[]{:S(2)}) async-start(), calls=%async_computation.1 | async-start | bytes 131072 | tf_op jit(solution)/shard_map/psum | solution.py:108
  9.4 21.6 %collective-permute-start = (bf16[17,3,1,64,128]{4,3,2,1,0:T(8,128)(2,1)}, bf16[17,3,1,64,128]{4,3,2,1,0:T(8,128)(2,1)S(1)}, u32[]{:S(2)}, u32[]{:S(2)}) collective-permute-start(bf16[17,3,1,64,128]{4,3,2,1,0:T(8,128)(2,1)} %get-tuple-element.20), channel_id=1, source_target_pairs={{0,8},{8,16},{16,24},{24,32},{32,40},{40,48},{48,56},{56,64},{64,7... | collective-permute-start | bytes 2506760 | tf_op jit(solution)/shard_map/ppermute | solution.py:14
  13.5 21.3 %collective-permute-start.1 = (bf16[17,3,1,64,128]{4,3,2,1,0:T(8,128)(2,1)}, bf16[17,3,1,64,128]{4,3,2,1,0:T(8,128)(2,1)S(1)}, u32[]{:S(2)}, u32[]{:S(2)}) collective-permute-start(bf16[17,3,1,64,128]{4,3,2,1,0:T(8,128)(2,1)} %get-tuple-element.21), channel_id=1, source_target_pairs={{8,0},{16,8},{24,16},{32,24},{40,32},{48,40},{56,48},{64,56},{72,6... | collective-permute-start | bytes 2506760 | tf_op jit(solution)/shard_map/ppermute | solution.py:17
  94.6 250.2 %copy-start.1 = (f32[6144,128]{1,0:T(8,128)S(1)}, f32[6144,128]{1,0:T(8,128)}, u32[]{:S(2)}) copy-start(f32[6144,128]{1,0:T(8,128)} %copy.16) | copy-start | bytes 9437188
Sparse Core Ops, SparseCore 0:
  92.3 244.9 all-reduce.1
where the time goes:
time: 358 us
  waiting for transfers between devices  262 us (73%)
  blocking collectives  43.4 us (12%)
  between operations  14.4 us (4%)
  local copies, waits for them, and re-layouts  11.3 us (3%)
  matrix products  11.3 us (3%)
  other arithmetic  10.6 us (3%)
  starting transfers between devices  5.35 us (1%)
    psum x1, waiting for transfers between devices, per_device(): gram_total = lax.psum(gram_local, ('slab', 'snap'))  243 us
    all_to_all x1, blocking collectives, per_device(): lax.all_to_all(pieces, 'snap', split_axis=3, concat_axis=0, tiled=True)  43.4 us
    ppermute x1, waiting for transfers between devices, with_halo(): lax.ppermute(lax.slice_in_dim(block, block.shape[dim] - width, None, axis...  15.1 us
  transfers between devices with their start and end apart: 3, of which 3 were waited for; matrix products, arithmetic and copies ran while one was open for 1% of the time, Pallas kernels for 0%

commit v1 on v0

v1 whole, which is shorter than its diff:
```python
import functools

import jax
import jax.numpy as jnp
from jax import lax
from jax.experimental import pallas as pl
from jax.experimental.pallas import tpu as pltpu
from jax.sharding import PartitionSpec as P

NSITER = 6
F32 = jnp.float32
BF16 = jnp.bfloat16
MESH = pl.DeviceIdType.MESH


def remote(src, dst, ssem, rsem, dev):
    return pltpu.make_async_remote_copy(
        src_ref=src, dst_ref=dst, send_sem=ssem, recv_sem=rsem, device_id=dev, device_id_type=MESH
    )


def wait_bytes(ref, sem):
    pltpu.make_async_copy(ref, ref, sem).wait()


def gather_kernel(
    flow_hbm, large_hbm, mod_hbm, metric_hbm,
    vh_hbm, vl_hbm, g_out,
    flow_v, flow_f, send, cols, halo, large_b, large_f, mod_v, mod_b, met,
    vh, vl, acc, gs, rx, ys, ry, zs, rz, ag, gf,
    in_sem, big_sem, xs_sem, xr_sem, hs_sem, hr_sem, ls_sem, lr_sem, v_sem, as_sem, ar_sem,
):
    slab = lax.axis_index("slab")
    i = lax.axis_index("snap")
    z = slab // 4
    y = lax.rem(slab, 4)
    up = lax.rem(slab + 1, 32)
    down = lax.rem(slab + 31, 32)

    flow_in = pltpu.make_async_copy(flow_hbm, flow_v, big_sem)
    flow_in.start()
    large_in = pltpu.make_async_copy(large_hbm, large_b, in_sem.at[0])
    large_in.start()
    mod_in = pltpu.make_async_copy(mod_hbm, mod_v, in_sem.at[1])
    mod_in.start()
    met_in = pltpu.make_async_copy(
        metric_hbm.at[:, :, pl.ds(pl.multiple_of(8 * i, 8), 8), :], met, in_sem.at[2]
    )
    met_in.start()

    snap_dev = [{"slab": slab, "snap": lax.rem(i + d, 8)} for d in range(1, 8)]
    y_dev = [{"slab": z * 4 + lax.rem(y + d, 4), "snap": i} for d in range(1, 4)]
    z_dev = [{"slab": lax.rem(z + d, 8) * 4 + y, "snap": i} for d in range(1, 8)]
    side_dev = [{"slab": down, "snap": i}, {"slab": up, "snap": i}]
    barrier = pltpu.get_barrier_semaphore()
    everyone = snap_dev + y_dev + z_dev + side_dev
    for dev in everyone:
        pl.semaphore_signal(barrier, inc=1, device_id=dev, device_id_type=MESH)

    large_in.wait()
    for c in range(3):
        for p in range(2):
            large_f[c, p + 1] = large_b[c, p].astype(F32)
    flow_in.wait()

    def widen(s, carry):
        flow_f[pl.ds(pl.multiple_of(s * 384, 384), 384), :] = flow_v[s].astype(F32)
        return carry

    lax.fori_loop(0, 16, widen, 0)

    def transpose(t):
        for b in range(8):
            for cy in range(6):
                tile = flow_f[pl.ds(cy * 64 + 8 * b + t, 16, stride=384), :]
                send[8 * b + t, cy // 2, cy % 2] = tile.astype(BF16)

    transpose(0)
    pl.semaphore_wait(barrier, len(everyone))

    mine16 = pl.ds(pl.multiple_of(16 * i, 16), 16)
    rows8 = pl.ds(pl.multiple_of(8 * i, 8), 8)
    large_copies = [
        remote(large_f.at[:, 1, rows8, :], large_f.at[:, 3, rows8, :], ls_sem.at[0], lr_sem.at[0], side_dev[0]),
        remote(large_f.at[:, 2, rows8, :], large_f.at[:, 0, rows8, :], ls_sem.at[1], lr_sem.at[1], side_dev[1]),
    ]
    for copy in large_copies:
        copy.start()

    def send_step(t, carry):
        @pl.when(t < 7)
        def _():
            transpose(t + 1)

        for d in range(1, 8):
            target = lax.rem(i + d, 8)
            remote(
                send.at[8 * target + t], cols.at[t + 1, :, :, mine16, :],
                xs_sem.at[t + 1], xr_sem.at[t + 1], {"slab": slab, "snap": target},
            ).start()
        pltpu.make_async_copy(
            send.at[8 * i + t], cols.at[t + 1, :, :, mine16, :], xr_sem.at[t + 1]
        ).start()
        return carry

    lax.fori_loop(0, 8, send_step, 0)
    for slot, shift in ((0, 63), (9, 8)):
        for d in range(1, 8):
            target = lax.rem(i + d, 8)
            remote(
                send.at[lax.rem(8 * target + shift, 64), pl.ds(1, 2)],
                cols.at[slot, pl.ds(1, 2), :, mine16, :],
                xs_sem.at[slot], xr_sem.at[slot], {"slab": slab, "snap": target},
            ).start()
        pltpu.make_async_copy(
            send.at[lax.rem(8 * i + shift, 64), pl.ds(1, 2)],
            cols.at[slot, pl.ds(1, 2), :, mine16, :], xr_sem.at[slot],
        ).start()

    mod_in.wait()

    def spread(k, carry):
        column = lax.rem(8 * i + k + 63, 64)
        mod_b[k] = jnp.broadcast_to(mod_v[pl.ds(column, 1), :], (128, 128)).T
        return carry

    lax.fori_loop(0, 10, spread, 0)
    met_in.wait()
    for copy in large_copies:
        copy.wait()

    @pl.when(slab == 0)
    def _():
        large_f[:, 0] = jnp.zeros((3, 64, 128), F32)

    @pl.when(slab == 31)
    def _():
        large_f[:, 3] = jnp.zeros((3, 64, 128), F32)

    acc[...] = jnp.zeros((128, 256), F32)

    def pass_on(xx):
        wait_bytes(cols.at[xx], xr_sem.at[xx])
        for side in range(2):
            remote(
                cols.at[xx, :, side], halo.at[1 - side, xx - 1],
                hs_sem.at[side, xx - 1], hr_sem.at[1 - side, xx - 1], side_dev[side],
            ).start()

    def pass_step(k, carry):
        pass_on(k + 1)
        return carry

    lax.fori_loop(0, 3, pass_step, 0)

    def write_out(xx):
        lanes = pl.ds(pl.multiple_of(128 * (xx - 1), 128), 128)
        pltpu.make_async_copy(vh.at[:, :, lanes], vh_hbm.at[:, :, lanes], v_sem.at[0]).start()
        pltpu.make_async_copy(vl.at[:, :, lanes], vl_hbm.at[:, :, lanes], v_sem.at[1]).start()

    def column(k, carry):
        xx = lax.rem(k + 1, 8) + 1

        @pl.when(k < 5)
        def _():
            pass_on(k + 4)

        @pl.when(k == 6)
        def _():
            wait_bytes(cols.at[0, pl.ds(1, 2)], xr_sem.at[0])
            wait_bytes(cols.at[9, pl.ds(1, 2)], xr_sem.at[9])

        for side in range(2):
            wait_bytes(halo.at[side, xx - 1], hr_sem.at[side, xx - 1])

        @pl.when(slab == 0)
        def _():
            halo[0, xx - 1] = jnp.zeros((3, 128, 128), BF16)

        @pl.when(slab == 31)
        def _():
            halo[1, xx - 1] = jnp.zeros((3, 128, 128), BF16)

        here = 8 * i + xx - 1
        before = lax.rem(here + 63, 64)
        after = lax.rem(here + 1, 64)
        base = [[large_f[c, p, pl.ds(here, 1), :] for p in range(4)] for c in range(3)]
        base_m = [[large_f[c, p + 1, pl.ds(before, 1), :] for p in range(2)] for c in (1, 2)]
        base_p = [[large_f[c, p + 1, pl.ds(after, 1), :] for p in range(2)] for c in (1, 2)]
        half = [[0.5 * met[m, p, pl.ds(xx - 1, 1), :] for p in range(2)] for m in range(4)]
        lanes = pl.ds(pl.multiple_of(128 * (xx - 1), 128), 128)

        def snaps(s, inner):
            r = pl.ds(pl.multiple_of(16 * s, 16), 16)
            m0 = mod_b[xx, r, :]
            mm = mod_b[xx - 1, r, :]
            mp = mod_b[xx + 1, r, :]

            def field(c):
                return [
                    halo[0, xx - 1, c, r, :].astype(F32) + m0 * base[c][0],
                    cols[xx, c, 0, r, :].astype(F32) + m0 * base[c][1],
                    cols[xx, c, 1, r, :].astype(F32) + m0 * base[c][2],
                    halo[1, xx - 1, c, r, :].astype(F32) + m0 * base[c][3],
                ]

            def along_x(c, p):
                right = cols[xx + 1, c, p, r, :].astype(F32) + mp * base_p[c - 1][p]
                left = cols[xx - 1, c, p, r, :].astype(F32) + mm * base_m[c - 1][p]
                return right - left

            def along_z(f):
                return pltpu.roll(f, 127, 1) - pltpu.roll(f, 1, 1)

            u, v, w = field(0), field(1), field(2)
            for p in range(2):
                gx, sxy, gy, gz = (half[m][p] for m in range(4))
                du = u[p + 2] - u[p]
                dv = v[p + 2] - v[p]
                dw = w[p + 2] - w[p]
                around = (
                    gy * dw - gz * along_z(v[p + 1]),
                    gz * along_z(u[p + 1]) - (gx * along_x(2, p) + sxy * dw),
                    (gx * along_x(1, p) + sxy * dv) - gy * du,
                )
                for c in range(3):
                    high = around[c].astype(BF16)
                    vh[2 * c + p, r, lanes] = high
                    vl[2 * c + p, r, lanes] = (around[c] - high.astype(F32)).astype(BF16)
            return inner

        lax.fori_loop(0, 8, snaps, 0)
        rows_h = jnp.concatenate([vh[cy, :, lanes] for cy in range(6)], axis=1)
        rows_l = jnp.concatenate([vl[cy, :, lanes] for cy in range(6)], axis=1)
        both = jnp.concatenate([rows_h, rows_l], axis=0)
        acc[...] += lax.dot_general(
            rows_h, both, (((1,), (1,)), ((), ())), preferred_element_type=F32
        )
        write_out(xx)
        return carry

    lax.fori_loop(0, 8, column, 0)
    gs[...] = 0.5 * acc[:, :128] + acc[:, 128:]

    def exchange(stage, src_of, dst, slot, devs, ids, width):
        for dev, target in zip(devs, ids):
            remote(src_of(target), dst.at[slot], as_sem.at[stage], ar_sem.at[stage], dev).start()
        pltpu.make_async_copy(src_of(slot_id[stage]), dst.at[slot], ar_sem.at[stage]).start()
        wait_bytes(dst, ar_sem.at[stage])

    slot_id = {0: i, 1: y, 2: z, 3: i}
    snap_ids = [lax.rem(i + d, 8) for d in range(1, 8)]

    def rows_of(k):
        return gs.at[pl.ds(pl.multiple_of(16 * k, 16), 16)]

    exchange(0, rows_of, rx, i, snap_dev, snap_ids, 8)
    ys[...] = jnp.sum(rx[...], axis=0)
    exchange(1, lambda k: ys, ry, y, y_dev, [None] * 3, 4)
    zs[...] = jnp.sum(ry[...], axis=0)
    exchange(2, lambda k: zs, rz, z, z_dev, [None] * 7, 8)
    ag[...] = jnp.sum(rz[...], axis=0)
    exchange(3, lambda k: ag, gf, i, snap_dev, [None] * 7, 8)
    g_out[...] = gf[...]

    for t in range(8):
        wait_bytes(send.at[pl.ds(0, 7)], xs_sem.at[t + 1])
    for slot in (0, 9):
        wait_bytes(send.at[pl.ds(0, 7), pl.ds(1, 2)], xs_sem.at[slot])
    for side in range(2):
        for k in range(8):
            wait_bytes(cols.at[k + 1, :, side], hs_sem.at[side, k])
    pltpu.make_async_copy(vh, vh_hbm, v_sem.at[0]).wait()
    pltpu.make_async_copy(vl, vl_hbm, v_sem.at[1]).wait()
    wait_bytes(rx.at[pl.ds(0, 7)], as_sem.at[0])
    wait_bytes(ry.at[pl.ds(0, 3)], as_sem.at[1])
    wait_bytes(rz.at[pl.ds(0, 7)], as_sem.at[2])
    wait_bytes(gf.at[pl.ds(0, 7)], as_sem.at[3])


def gather(flow, large, mod_t, metric):
    any_space = pl.BlockSpec(memory_space=pl.ANY)
    dma = pltpu.SemaphoreType.DMA
    return pl.pallas_call(
        gather_kernel,
        name="gather",
        out_shape=(
            jax.ShapeDtypeStruct((6, 128, 1024), BF16),
            jax.ShapeDtypeStruct((6, 128, 1024), BF16),
            jax.ShapeDtypeStruct((8, 16, 128), F32),
        ),
        in_specs=[any_space] * 4,
        out_specs=(any_space, any_space, pl.BlockSpec(memory_space=pltpu.VMEM)),
        scratch_shapes=[
            pltpu.VMEM((16, 384, 128), BF16),
            pltpu.VMEM((6144, 128), F32),
            pltpu.VMEM((64, 3, 2, 16, 128), BF16),
            pltpu.VMEM((10, 3, 2, 128, 128), BF16),
            pltpu.VMEM((2, 8, 3, 128, 128), BF16),
            pltpu.VMEM((3, 2, 64, 128), BF16),
            pltpu.VMEM((3, 4, 64, 128), F32),
            pltpu.VMEM((64, 128), F32),
            pltpu.VMEM((10, 128, 128), F32),
            pltpu.VMEM((4, 2, 8, 128), F32),
            pltpu.VMEM((6, 128, 1024), BF16),
            pltpu.VMEM((6, 128, 1024), BF16),
            pltpu.VMEM((128, 256), F32),
            pltpu.VMEM((128, 128), F32),
            pltpu.VMEM((8, 16, 128), F32),
            pltpu.VMEM((16, 128), F32),
            pltpu.VMEM((4, 16, 128), F32),
            pltpu.VMEM((16, 128), F32),
            pltpu.VMEM((8, 16, 128), F32),
            pltpu.VMEM((16, 128), F32),
            pltpu.VMEM((8, 16, 128), F32),
            dma((3,)), dma, dma((10,)), dma((10,)), dma((2, 8)), dma((2, 8)),
            dma((2,)), dma((2,)), dma((2,)), dma((4,)), dma((4,)),
        ],
        compiler_params=pltpu.CompilerParams(collective_id=0, has_side_effects=True),
    )(flow, large, mod_t, metric)


def whiten_kernel(cells, vh_hbm, vl_hbm, g_ref, out_hbm, vh, vl, out_v, in_sem, out_sem):
    loads = [
        [
            pltpu.make_async_copy(vh_hbm.at[k], vh.at[k], in_sem.at[0, k]),
            pltpu.make_async_copy(vl_hbm.at[k], vl.at[k], in_sem.at[1, k]),
        ]
        for k in range(6)
    ]
    for pair in loads:
        for copy in pair:
            copy.start()

    half = g_ref[...]
    correlation = (half + half.T) / cells
    eye = (
        lax.broadcasted_iota(jnp.int32, (128, 128), 0) == lax.broadcasted_iota(jnp.int32, (128, 128), 1)
    ).astype(F32)
    frob_scale = jnp.sqrt(jnp.sum(correlation * correlation, keepdims=True) + 1e-06)
    dot = functools.partial(jnp.dot, precision=lax.Precision.HIGHEST, preferred_element_type=F32)
    approx = correlation / frob_scale
    factor = 0.5 * (3.0 * eye - approx)
    approx = dot(approx, factor)
    inverse = factor
    for repeat in range(1, NSITER):
        factor = 0.5 * (3.0 * eye - dot(inverse, approx))
        if repeat < NSITER - 1:
            approx = dot(approx, factor)
        inverse = dot(factor, inverse)
    weights = inverse / jnp.sqrt(frob_scale)
    w_high = weights.astype(BF16)
    w_low = (weights - w_high.astype(F32)).astype(BF16)

    stores = []
    for k in range(6):
        for copy in loads[k]:
            copy.wait()
        high = vh[k]
        result = jnp.dot(w_high, high, preferred_element_type=F32)
        result += jnp.dot(w_high, vl[k], preferred_element_type=F32)
        result += jnp.dot(w_low, high, preferred_element_type=F32)
        for x in range(8):
            out_v[k, pl.ds(x, 128, stride=8), :] = result[:, 128 * x : 128 * (x + 1)]
        store = pltpu.make_async_copy(
            out_v.at[k].reshape(128, 8, 128), out_hbm.at[:, k // 2, k % 2], out_sem.at[k]
        )
        store.start()
        stores.append(store)
    for store in stores:
        store.wait()


def whiten(vh, vl, gram, cells):
    any_space = pl.BlockSpec(memory_space=pl.ANY)
    dma = pltpu.SemaphoreType.DMA
    return pl.pallas_call(
        functools.partial(whiten_kernel, cells),
        name="whiten",
        out_shape=jax.ShapeDtypeStruct((128, 3, 2, 8, 128), F32),
        in_specs=[any_space, any_space, pl.BlockSpec(memory_space=pltpu.VMEM)],
        out_specs=any_space,
        scratch_shapes=[
            pltpu.VMEM((6, 128, 1024), BF16),
            pltpu.VMEM((6, 128, 1024), BF16),
            pltpu.VMEM((6, 1024, 128), F32),
            dma((2, 6)),
            dma((6,)),
        ],
    )(vh, vl, gram)


def per_device(flow, large_scale, modulation, metric):
    vh, vl, gram = gather(flow.reshape(16, 384, 128), large_scale, modulation.T, metric)
    return whiten(vh, vl, gram.reshape(128, 128), 3.0 * 64 * 64 * 128)


def solution(mesh):
    return jax.shard_map(
        per_device,
        mesh=mesh,
        in_specs=(
            P("snap", None, "slab", None, None),
            P(None, "slab", None, None),
            P(),
            P(None, "slab", None, None),
        ),
        out_specs=P(None, None, "slab", "snap", None),
        check_vma=False,
    )
```

time: 358 us -> 63.1 us (0.18)
  waiting for transfers between devices: 262 us -> 0 us
  Pallas kernels: 0 us -> 62.9 us
  blocking collectives: 43.4 us -> 0 us
  between operations: 14.4 us -> 0.01 us
  matrix products: 11.3 us -> 0 us
  local copies, waits for them, and re-layouts: 11.3 us -> 0 us
  other arithmetic: 10.6 us -> 0 us
  starting transfers between devices: 5.35 us -> 0 us
    psum x1 -> x0, waiting for transfers between devices: 243 us -> none  [per_device(): gram_total = lax.psum(gram_local, ('slab', 'snap'))]
    pallas_call x0 -> x2, Pallas kernels: none -> 62.9 us  [the longest x1 55.3 us: gather(): pl.pallas_call(gather_kernel, name='gather', out_shape=(jax.ShapeDtypeStr...]
    all_to_all x1 -> x0, blocking collectives: 43.4 us -> none  [per_device(): lax.all_to_all(pieces, 'snap', split_axis=3, concat_axis=0, tiled=True)]
    ppermute x2 -> x0, waiting for transfers between devices: 18.9 us -> none  [the longest x1 15.1 us: with_halo(): lax.ppermute(lax.slice_in_dim(block, block.shape[dim] - width, None, axis...]
    dot_general x19 -> x0, matrix products: 11.3 us -> none  [the longest x1 3.23 us: inner_rows(): lax.dot_general(left_rows, right_rows, (((1,), (1,)), ((), ())), precisio...]
    dot_general x2 -> x0, local copies, waits for them, and re-layouts: 5.85 us -> none  [per_device(): result = jnp.dot(weights, snapshot_rows, precision=lax.Precision.HIGHEST)]
    ppermute x2 -> x0, starting transfers between devices: 5.35 us -> none  [the longest x1 4.06 us: with_halo(): lax.ppermute(lax.slice_in_dim(block, block.shape[dim] - width, None, axis...]
  transfers between devices with their start and end apart: 3 -> 0, of which waited for: 3 -> 0; matrix products, arithmetic and copies ran while one was open for 1% -> 0% of each run, Pallas kernels for 0% -> 0%
where the time goes in v1:
time: 63.1 us; the launch traced here: 62.9 us
  Pallas kernels  62.9 us (100%)
    pallas_call x1, Pallas kernels, gather(): pl.pallas_call(gather_kernel, name='gather', out_shape=(jax.ShapeDtypeStr...  55.3 us
    pallas_call x1, Pallas kernels, whiten(): pl.pallas_call(functools.partial(whiten_kernel, cells), name='whiten', ou...  7.68 us

profile of v1, /device:TPU:1, one launch (start us, length us, event | category | flops | bytes accessed | tf_op | source)
XLA Modules:
  0.0 62.9 jit_solution(8882945653319140556)
XLA Ops:
  0.0 55.3 %gather.1 = (bf16[6,128,1024]{2,1,0:T(8,128)(2,1)}, bf16[6,128,1024]{2,1,0:T(8,128)(2,1)}, f32[8,16,128]{2,1,0:T(8,128)}) custom-call(bf16[16,384,128]{2,1,0:T(8,128)(2,1)} %bitcast.3, bf16[3,2,64,128]{3,2,1,0:T(8,128)(2,1)} %large_hbm.1, f32[64,128]{1,0:T(8,128)} %bitcast.5, f32[4,2,64,128]{3,2,1,0:T(8,128)} %metric_hbm.1), custom_call_target="tpu_custom_call" | custom-call | tf_op jit(solution)/shard_map/gather/pallas_call | solution.py:284
  55.3 7.7 %whiten.1 = f32[128,3,2,8,128]{4,3,2,1,0:T(8,128)} custom-call(bf16[6,128,1024]{2,1,0:T(8,128)(2,1)} %get-tuple-element.8.vh_hbm, bf16[6,128,1024]{2,1,0:T(8,128)(2,1)} %get-tuple-element.9.vl_hbm, f32[128,128]{1,0:T(8,128)} %bitcast.4), custom_call_target="tpu_custom_call" | custom-call | tf_op jit(solution)/shard_map/whiten/pallas_call | solution.py:377

commit v2 on v1

--- a/solution.py
+++ b/solution.py
@@ -25,10 +25,10 @@
 
 def gather_kernel(
     flow_hbm, large_hbm, mod_hbm, metric_hbm,
-    vh_hbm, vl_hbm, g_out,
+    vh, vl, g_out,
     flow_v, flow_f, send, cols, halo, large_b, large_f, mod_v, mod_b, met,
-    vh, vl, acc, gs, rx, ys, ry, zs, rz, ag, gf,
-    in_sem, big_sem, xs_sem, xr_sem, hs_sem, hr_sem, ls_sem, lr_sem, v_sem, as_sem, ar_sem,
+    acc, gs, rx, zs, rz, ag, gf,
+    in_sem, big_sem, xs_sem, xr_sem, hs_sem, hr_sem, ls_sem, lr_sem, as_sem, ar_sem,
 ):
     slab = lax.axis_index("slab")
     i = lax.axis_index("snap")
@@ -48,14 +48,32 @@
     )
     met_in.start()
 
-    snap_dev = [{"slab": slab, "snap": lax.rem(i + d, 8)} for d in range(1, 8)]
-    y_dev = [{"slab": z * 4 + lax.rem(y + d, 4), "snap": i} for d in range(1, 4)]
-    z_dev = [{"slab": lax.rem(z + d, 8) * 4 + y, "snap": i} for d in range(1, 8)]
+    q = 8 * y + i
+
+    def plane_dev(k):
+        return {"slab": z * 4 + k // 8, "snap": lax.rem(k, 8)}
+
+    def column_dev(k):
+        return {"slab": k * 4 + y, "snap": i}
+
     side_dev = [{"slab": down, "snap": i}, {"slab": up, "snap": i}]
     barrier = pltpu.get_barrier_semaphore()
-    everyone = snap_dev + y_dev + z_dev + side_dev
-    for dev in everyone:
+
+    def greet(dev):
         pl.semaphore_signal(barrier, inc=1, device_id=dev, device_id_type=MESH)
+
+    def greet_plane(d, carry):
+        greet(plane_dev(lax.rem(q + d, 32)))
+        return carry
+
+    def greet_column(d, carry):
+        greet(column_dev(lax.rem(z + d, 8)))
+        return carry
+
+    lax.fori_loop(1, 8, greet_column, 0)
+    lax.fori_loop(1, 32, greet_plane, 0)
+    for dev in side_dev:
+        greet(dev)
 
     large_in.wait()
     for c in range(3):
@@ -76,7 +94,7 @@
                 send[8 * b + t, cy // 2, cy % 2] = tile.astype(BF16)
 
     transpose(0)
-    pl.semaphore_wait(barrier, len(everyone))
+    pl.semaphore_wait(barrier, 31 + 7 + 2)
 
     mine16 = pl.ds(pl.multiple_of(16 * i, 16), 16)
     rows8 = pl.ds(pl.multiple_of(8 * i, 8), 8)
@@ -152,11 +170,6 @@
         return carry
 
     lax.fori_loop(0, 3, pass_step, 0)
-
-    def write_out(xx):
-        lanes = pl.ds(pl.multiple_of(128 * (xx - 1), 128), 128)
-        pltpu.make_async_copy(vh.at[:, :, lanes], vh_hbm.at[:, :, lanes], v_sem.at[0]).start()
-        pltpu.make_async_copy(vl.at[:, :, lanes], vl_hbm.at[:, :, lanes], v_sem.at[1]).start()
 
     def column(k, carry):
         xx = lax.rem(k + 1, 8) + 1
@@ -236,31 +249,30 @@
         acc[...] += lax.dot_general(
             rows_h, both, (((1,), (1,)), ((), ())), preferred_element_type=F32
         )
-        write_out(xx)
         return carry
 
     lax.fori_loop(0, 8, column, 0)
-    gs[...] = 0.5 * acc[:, :128] + acc[:, 128:]
-
-    def exchange(stage, src_of, dst, slot, devs, ids, width):
-        for dev, target in zip(devs, ids):
-            remote(src_of(target), dst.at[slot], as_sem.at[stage], ar_sem.at[stage], dev).start()
-        pltpu.make_async_copy(src_of(slot_id[stage]), dst.at[slot], ar_sem.at[stage]).start()
+    half_gram = 0.5 * acc[:, :128] + acc[:, 128:]
+    for k in range(32):
+        gs[k] = half_gram[4 * k : 4 * k + 4, :]
+
+    def exchange(stage, count, mine, device_of, src_of, dst):
+        def one(d, carry):
+            target = lax.rem(mine + d, count)
+            remote(
+                src_of(target), dst.at[mine], as_sem.at[stage], ar_sem.at[stage], device_of(target)
+            ).start()
+            return carry
+
+        lax.fori_loop(1, count, one, 0)
+        pltpu.make_async_copy(src_of(mine), dst.at[mine], ar_sem.at[stage]).start()
         wait_bytes(dst, ar_sem.at[stage])
 
-    slot_id = {0: i, 1: y, 2: z, 3: i}
-    snap_ids = [lax.rem(i + d, 8) for d in range(1, 8)]
-
-    def rows_of(k):
-        return gs.at[pl.ds(pl.multiple_of(16 * k, 16), 16)]
-
-    exchange(0, rows_of, rx, i, snap_dev, snap_ids, 8)
-    ys[...] = jnp.sum(rx[...], axis=0)
-    exchange(1, lambda k: ys, ry, y, y_dev, [None] * 3, 4)
-    zs[...] = jnp.sum(ry[...], axis=0)
-    exchange(2, lambda k: zs, rz, z, z_dev, [None] * 7, 8)
+    exchange(0, 32, q, plane_dev, lambda k: gs.at[k], rx)
+    zs[...] = jnp.sum(rx[...], axis=0)
+    exchange(1, 8, z, column_dev, lambda k: zs, rz)
     ag[...] = jnp.sum(rz[...], axis=0)
-    exchange(3, lambda k: ag, gf, i, snap_dev, [None] * 7, 8)
+    exchange(2, 32, q, plane_dev, lambda k: ag, gf)
     g_out[...] = gf[...]
 
     for t in range(8):
@@ -270,27 +282,24 @@
     for side in range(2):
         for k in range(8):
             wait_bytes(cols.at[k + 1, :, side], hs_sem.at[side, k])
-    pltpu.make_async_copy(vh, vh_hbm, v_sem.at[0]).wait()
-    pltpu.make_async_copy(vl, vl_hbm, v_sem.at[1]).wait()
-    wait_bytes(rx.at[pl.ds(0, 7)], as_sem.at[0])
-    wait_bytes(ry.at[pl.ds(0, 3)], as_sem.at[1])
-    wait_bytes(rz.at[pl.ds(0, 7)], as_sem.at[2])
-    wait_bytes(gf.at[pl.ds(0, 7)], as_sem.at[3])
+    wait_bytes(rx.at[pl.ds(0, 31)], as_sem.at[0])
+    wait_bytes(rz.at[pl.ds(0, 7)], as_sem.at[1])
+    wait_bytes(gf.at[pl.ds(0, 31)], as_sem.at[2])
 
 
 def gather(flow, large, mod_t, metric):
-    any_space = pl.BlockSpec(memory_space=pl.ANY)
+    vmem = pl.BlockSpec(memory_space=pltpu.VMEM)
     dma = pltpu.SemaphoreType.DMA
     return pl.pallas_call(
         gather_kernel,
         name="gather",
         out_shape=(
-            jax.ShapeDtypeStruct((6, 128, 1024), BF16),
-            jax.ShapeDtypeStruct((6, 128, 1024), BF16),
-            jax.ShapeDtypeStruct((8, 16, 128), F32),
+            pltpu.VMEM((6, 128, 1024), BF16),
+            pltpu.VMEM((6, 128, 1024), BF16),
+            pltpu.VMEM((32, 4, 128), F32),
         ),
-        in_specs=[any_space] * 4,
-        out_specs=(any_space, any_space, pl.BlockSpec(memory_space=pltpu.VMEM)),
+        in_specs=[pl.BlockSpec(memory_space=pltpu.HBM)] * 4,
+        out_specs=(vmem, vmem, vmem),
         scratch_shapes=[
             pltpu.VMEM((16, 384, 128), BF16),
             pltpu.VMEM((6144, 128), F32),
@@ -302,43 +311,41 @@
             pltpu.VMEM((64, 128), F32),
             pltpu.VMEM((10, 128, 128), F32),
             pltpu.VMEM((4, 2, 8, 128), F32),
-            pltpu.VMEM((6, 128, 1024), BF16),
-            pltpu.VMEM((6, 128, 1024), BF16),
             pltpu.VMEM((128, 256), F32),
-            pltpu.VMEM((128, 128), F32),
-            pltpu.VMEM((8, 16, 128), F32),
-            pltpu.VMEM((16, 128), F32),
-            pltpu.VMEM((4, 16, 128), F32),
-            pltpu.VMEM((16, 128), F32),
-            pltpu.VMEM((8, 16, 128), F32),
-            pltpu.VMEM((16, 128), F32),
-            pltpu.VMEM((8, 16, 128), F32),
+            pltpu.VMEM((32, 4, 128), F32),
+            pltpu.VMEM((32, 4, 128), F32),
+            pltpu.VMEM((4, 128), F32),
+            pltpu.VMEM((8, 4, 128), F32),
+            pltpu.VMEM((4, 128), F32),
+            pltpu.VMEM((32, 4, 128), F32),
             dma((3,)), dma, dma((10,)), dma((10,)), dma((2, 8)), dma((2, 8)),
-            dma((2,)), dma((2,)), dma((2,)), dma((4,)), dma((4,)),
+            dma((2,)), dma((2,)), dma((3,)), dma((3,)),
         ],
-        compiler_params=pltpu.CompilerParams(collective_id=0, has_side_effects=True),
+        compiler_params=pltpu.CompilerParams(
+            collective_id=0, has_side_effects=True, vmem_limit_bytes=32 << 20
+        ),
     )(flow, large, mod_t, metric)
 
 
-def whiten_kernel(cells, vh_hbm, vl_hbm, g_ref, out_hbm, vh, vl, out_v, in_sem, out_sem):
-    loads = [
-        [
-            pltpu.make_async_copy(vh_hbm.at[k], vh.at[k], in_sem.at[0, k]),
-            pltpu.make_async_copy(vl_hbm.at[k], vl.at[k], in_sem.at[1, k]),
-        ]
-        for k in range(6)
-    ]
-    for pair in loads:
-        for copy in pair:
-            copy.start()
-
-    half = g_ref[...]
+def whiten_kernel(cells, vh, vl, g_ref, out_hbm, out_v, out_sem):
+    half = g_ref[...].reshape(128, 128)
     correlation = (half + half.T) / cells
     eye = (
         lax.broadcasted_iota(jnp.int32, (128, 128), 0) == lax.broadcasted_iota(jnp.int32, (128, 128), 1)
     ).astype(F32)
     frob_scale = jnp.sqrt(jnp.sum(correlation * correlation, keepdims=True) + 1e-06)
-    dot = functools.partial(jnp.dot, precision=lax.Precision.HIGHEST, preferred_element_type=F32)
+
+    def halves(a):
+        high = a.astype(BF16)
+        return high, (a - high.astype(F32)).astype(BF16)
+
+    def dot(a, b):
+        a_high, a_low = halves(a)
+        b_high, b_low = halves(b)
+        left = jnp.concatenate([a_high, a_high, a_low], axis=1)
+        right = jnp.concatenate([b_high, b_low, b_high], axis=0)
+        return jnp.dot(left, right, preferred_element_type=F32)
+
     approx = correlation / frob_scale
     factor = 0.5 * (3.0 * eye - approx)
     approx = dot(approx, factor)
@@ -354,8 +361,6 @@
 
     stores = []
     for k in range(6):
-        for copy in loads[k]:
-            copy.wait()
         high = vh[k]
         result = jnp.dot(w_high, high, preferred_element_type=F32)
         result += jnp.dot(w_high, vl[k], preferred_element_type=F32)
@@ -372,27 +377,22 @@
 
 
 def whiten(vh, vl, gram, cells):
-    any_space = pl.BlockSpec(memory_space=pl.ANY)
-    dma = pltpu.SemaphoreType.DMA
+    vmem = pl.BlockSpec(memory_space=pltpu.VMEM)
     return pl.pallas_call(
         functools.partial(whiten_kernel, cells),
         name="whiten",
         out_shape=jax.ShapeDtypeStruct((128, 3, 2, 8, 128), F32),
-        in_specs=[any_space, any_space, pl.BlockSpec(memory_space=pltpu.VMEM)],
-        out_specs=any_space,
-        scratch_shapes=[
-            pltpu.VMEM((6, 128, 1024), BF16),
-            pltpu.VMEM((6, 128, 1024), BF16),
-            pltpu.VMEM((6, 1024, 128), F32),
-            dma((2, 6)),
-            dma((6,)),
-        ],
+        in_specs=[vmem, vmem, vmem],
+        out_specs=pl.BlockSpec(memory_space=pl.ANY),
+        scratch_shapes=[pltpu.VMEM((6, 1024, 128), F32), pltpu.SemaphoreType.DMA((6,))],
+        compiler_params=pltpu.CompilerParams(vmem_limit_bytes=32 << 20),
     )(vh, vl, gram)
 
 
 def per_device(flow, large_scale, modulation, metric):
-    vh, vl, gram = gather(flow.reshape(16, 384, 128), large_scale, modulation.T, metric)
-    return whiten(vh, vl, gram.reshape(128, 128), 3.0 * 64 * 64 * 128)
+    sources = (flow.reshape(16, 384, 128), large_scale, modulation.T, metric)
+    vh, vl, gram = gather(*(pltpu.with_memory_space_constraint(a, pltpu.HBM) for a in sources))
+    return whiten(vh, vl, gram, 3.0 * 64 * 64 * 128)
 
 
 def solution(mesh):

time: 63.1 us -> 58.8 us (0.932)
  Pallas kernels: 62.9 us -> 58.7 us
    pallas_call x1, Pallas kernels: 7.68 us -> 4.26 us  [whiten(): pl.pallas_call(functools.partial(whiten_kernel, cells), name='whiten', ou...]
    pallas_call x1, Pallas kernels: 55.3 us -> 54.4 us  [gather(): pl.pallas_call(gather_kernel, name='gather', out_shape=(pltpu.VMEM((6, 12...]
where the time goes in v2:
time: 58.8 us; the launch traced here: 58.7 us
  Pallas kernels  58.7 us (100%)
    pallas_call x1, Pallas kernels, gather(): pl.pallas_call(gather_kernel, name='gather', out_shape=(pltpu.VMEM((6, 12...  54.4 us
    pallas_call x1, Pallas kernels, whiten(): pl.pallas_call(functools.partial(whiten_kernel, cells), name='whiten', ou...  4.26 us

profile of v2, /device:TPU:1, one launch (start us, length us, event | category | flops | bytes accessed | tf_op | source)
XLA Modules:
  0.0 58.7 jit_solution(4593918738451111028)
XLA Ops:
  0.0 54.4 %gather.1 = (bf16[6,128,1024]{2,1,0:T(8,128)(2,1)S(1)}, bf16[6,128,1024]{2,1,0:T(8,128)(2,1)S(1)}, f32[32,4,128]{2,1,0:T(4,128)S(1)}) custom-call(bf16[16,384,128]{2,1,0:T(8,128)(2,1)} %bitcast.2, bf16[3,2,64,128]{3,2,1,0:T(8,128)(2,1)} %large_hbm.1, f32[64,128]{1,0:T(8,128)} %bitcast.3, f32[4,2,64,128]{3,2,1,0:T(8,128)} %metric_hbm.1), custom_call_target="tpu_custom_call" | custom-call | tf_op jit(solution)/shard_map/gather/pallas_call | solution.py:293
  54.4 4.3 %whiten.1 = f32[128,3,2,8,128]{4,3,2,1,0:T(8,128)} custom-call(bf16[6,128,1024]{2,1,0:T(8,128)(2,1)S(1)} %get-tuple-element.8.vh, bf16[6,128,1024]{2,1,0:T(8,128)(2,1)S(1)} %get-tuple-element.9.vl, f32[32,4,128]{2,1,0:T(4,128)S(1)} %get-tuple-element.10.g_ref), custom_call_target="tpu_custom_call" | custom-call | tf_op jit(solution)/shard_map/whiten/pallas_call | solution.py:381

commit v3 on v2

--- a/solution.py
+++ b/solution.py
@@ -28,7 +28,7 @@
     vh, vl, g_out,
     flow_v, flow_f, send, cols, halo, large_b, large_f, mod_v, mod_b, met,
     acc, gs, rx, zs, rz, ag, gf,
-    in_sem, big_sem, xs_sem, xr_sem, hs_sem, hr_sem, ls_sem, lr_sem, as_sem, ar_sem,
+    in_sem, big_sem, xs_sem, xr_sem, hs_sem, hr_sem, ls_sem, lr_sem, as_sem, ar_sem, tokens,
 ):
     slab = lax.axis_index("slab")
     i = lax.axis_index("snap")
@@ -37,8 +37,25 @@
     up = lax.rem(slab + 1, 32)
     down = lax.rem(slab + 31, 32)
 
-    flow_in = pltpu.make_async_copy(flow_hbm, flow_v, big_sem)
-    flow_in.start()
+    q = 8 * y + i
+    side_dev = [{"slab": down, "snap": i}, {"slab": up, "snap": i}]
+    z_side = [{"slab": lax.rem(slab + 4, 32), "snap": i}, {"slab": lax.rem(slab + 28, 32), "snap": i}]
+    row_order = (4, 5, 2, 3, 6, 7, 1)
+    row_dev = [{"slab": slab, "snap": i ^ d} for d in row_order]
+    y_dev = [{"slab": slab ^ d, "snap": i} for d in (2, 1, 3)]
+    barrier = pltpu.get_barrier_semaphore()
+    greeted = row_dev + y_dev + side_dev + z_side
+    for dev in greeted:
+        pl.semaphore_signal(barrier, inc=1, device_id=dev, device_id_type=MESH)
+
+    flow_in = [
+        pltpu.make_async_copy(
+            flow_hbm.at[pl.ds(4 * k, 4)], flow_v.at[pl.ds(4 * k, 4)], big_sem.at[k]
+        )
+        for k in range(4)
+    ]
+    for copy in flow_in:
+        copy.start()
     large_in = pltpu.make_async_copy(large_hbm, large_b, in_sem.at[0])
     large_in.start()
     mod_in = pltpu.make_async_copy(mod_hbm, mod_v, in_sem.at[1])
@@ -48,70 +65,37 @@
     )
     met_in.start()
 
-    q = 8 * y + i
-
-    def plane_dev(k):
-        return {"slab": z * 4 + k // 8, "snap": lax.rem(k, 8)}
-
-    def column_dev(k):
-        return {"slab": k * 4 + y, "snap": i}
-
-    side_dev = [{"slab": down, "snap": i}, {"slab": up, "snap": i}]
-    barrier = pltpu.get_barrier_semaphore()
-
-    def greet(dev):
-        pl.semaphore_signal(barrier, inc=1, device_id=dev, device_id_type=MESH)
-
-    def greet_plane(d, carry):
-        greet(plane_dev(lax.rem(q + d, 32)))
+    def widen(s, carry):
+        for cy in range(6):
+            for b in range(8):
+                row = pl.multiple_of((cy * 8 + b) * 128 + 8 * s, 8)
+                flow_f[pl.ds(row, 8), :] = flow_v[s, pl.ds(cy * 64 + 8 * b, 8), :].astype(F32)
         return carry
 
-    def greet_column(d, carry):
-        greet(column_dev(lax.rem(z + d, 8)))
-        return carry
-
-    lax.fori_loop(1, 8, greet_column, 0)
-    lax.fori_loop(1, 32, greet_plane, 0)
-    for dev in side_dev:
-        greet(dev)
-
-    large_in.wait()
-    for c in range(3):
-        for p in range(2):
-            large_f[c, p + 1] = large_b[c, p].astype(F32)
-    flow_in.wait()
-
-    def widen(s, carry):
-        flow_f[pl.ds(pl.multiple_of(s * 384, 384), 384), :] = flow_v[s].astype(F32)
-        return carry
-
-    lax.fori_loop(0, 16, widen, 0)
+    for k in range(4):
+        flow_in[k].wait()
+        lax.fori_loop(4 * k, 4 * k + 4, widen, 0)
 
     def transpose(t):
         for b in range(8):
             for cy in range(6):
-                tile = flow_f[pl.ds(cy * 64 + 8 * b + t, 16, stride=384), :]
+                tile = flow_f[pl.ds((cy * 8 + b) * 128 + t, 16, stride=8), :]
                 send[8 * b + t, cy // 2, cy % 2] = tile.astype(BF16)
 
     transpose(0)
-    pl.semaphore_wait(barrier, 31 + 7 + 2)
+    pl.semaphore_wait(barrier, len(greeted))
+    for dev in z_side:
+        pl.semaphore_signal(tokens.at[0], inc=1, device_id=dev, device_id_type=MESH)
 
     mine16 = pl.ds(pl.multiple_of(16 * i, 16), 16)
     rows8 = pl.ds(pl.multiple_of(8 * i, 8), 8)
-    large_copies = [
-        remote(large_f.at[:, 1, rows8, :], large_f.at[:, 3, rows8, :], ls_sem.at[0], lr_sem.at[0], side_dev[0]),
-        remote(large_f.at[:, 2, rows8, :], large_f.at[:, 0, rows8, :], ls_sem.at[1], lr_sem.at[1], side_dev[1]),
-    ]
-    for copy in large_copies:
-        copy.start()
-
     def send_step(t, carry):
         @pl.when(t < 7)
         def _():
             transpose(t + 1)
 
-        for d in range(1, 8):
-            target = lax.rem(i + d, 8)
+        for d in row_order:
+            target = i ^ d
             remote(
                 send.at[8 * target + t], cols.at[t + 1, :, :, mine16, :],
                 xs_sem.at[t + 1], xr_sem.at[t + 1], {"slab": slab, "snap": target},
@@ -123,8 +107,8 @@
 
     lax.fori_loop(0, 8, send_step, 0)
     for slot, shift in ((0, 63), (9, 8)):
-        for d in range(1, 8):
-            target = lax.rem(i + d, 8)
+        for d in row_order:
+            target = i ^ d
             remote(
                 send.at[lax.rem(8 * target + shift, 64), pl.ds(1, 2)],
                 cols.at[slot, pl.ds(1, 2), :, mine16, :],
@@ -135,6 +119,13 @@
             cols.at[slot, pl.ds(1, 2), :, mine16, :], xr_sem.at[slot],
         ).start()
 
+    large_in.wait()
+    for c in range(3):
+        for p in range(2):
+            large_f[c, p + 1] = large_b[c, p].astype(F32)
+    pl.semaphore_wait(tokens.at[0], 2)
+    for dev in z_side:
+        pl.semaphore_signal(tokens.at[1], inc=1, device_id=dev, device_id_type=MESH)
     mod_in.wait()
 
     def spread(k, carry):
@@ -143,18 +134,17 @@
         return carry
 
     lax.fori_loop(0, 10, spread, 0)
+    large_copies = [
+        remote(large_f.at[:, 1, rows8, :], large_f.at[:, 3, rows8, :], ls_sem.at[0], lr_sem.at[0], side_dev[0]),
+        remote(large_f.at[:, 2, rows8, :], large_f.at[:, 0, rows8, :], ls_sem.at[1], lr_sem.at[1], side_dev[1]),
+    ]
+    for copy in large_copies:
+        copy.start()
+
+    pl.semaphore_wait(tokens.at[1], 2)
+    for dev in z_side:
+        pl.semaphore_signal(tokens.at[2], inc=1, device_id=dev, device_id_type=MESH)
     met_in.wait()
-    for copy in large_copies:
-        copy.wait()
-
-    @pl.when(slab == 0)
-    def _():
-        large_f[:, 0] = jnp.zeros((3, 64, 128), F32)
-
-    @pl.when(slab == 31)
-    def _():
-        large_f[:, 3] = jnp.zeros((3, 64, 128), F32)
-
     acc[...] = jnp.zeros((128, 256), F32)
 
     def pass_on(xx):
@@ -170,6 +160,17 @@
         return carry
 
     lax.fori_loop(0, 3, pass_step, 0)
+    for copy in large_copies:
+        copy.wait()
+
+    @pl.when(slab == 0)
+    def _():
+        large_f[:, 0] = jnp.zeros((3, 64, 128), F32)
+
+    @pl.when(slab == 31)
+    def _():
+        large_f[:, 3] = jnp.zeros((3, 64, 128), F32)
+
 
     def column(k, carry):
         xx = lax.rem(k + 1, 8) + 1
@@ -242,7 +243,7 @@
                     vl[2 * c + p, r, lanes] = (around[c] - high.astype(F32)).astype(BF16)
             return inner
 
-        lax.fori_loop(0, 8, snaps, 0)
+        lax.fori_loop(0, 8, snaps, 0, unroll=2)
         rows_h = jnp.concatenate([vh[cy, :, lanes] for cy in range(6)], axis=1)
         rows_l = jnp.concatenate([vl[cy, :, lanes] for cy in range(6)], axis=1)
         both = jnp.concatenate([rows_h, rows_l], axis=0)
@@ -256,23 +257,22 @@
     for k in range(32):
         gs[k] = half_gram[4 * k : 4 * k + 4, :]
 
-    def exchange(stage, count, mine, device_of, src_of, dst):
-        def one(d, carry):
-            target = lax.rem(mine + d, count)
-            remote(
-                src_of(target), dst.at[mine], as_sem.at[stage], ar_sem.at[stage], device_of(target)
-            ).start()
-            return carry
-
-        lax.fori_loop(1, count, one, 0)
+    plane_order = sorted(range(1, 32), key=lambda d: -(2 * ((d >> 4) & 1) + 2 * ((d >> 2) & 1) + ((d >> 3) & 1) + ((d >> 1) & 1)))
+    plane = [(q ^ d, {"slab": slab ^ (d >> 3), "snap": i ^ (d & 7)}) for d in plane_order]
+    line = [(z ^ d, {"slab": slab ^ (4 * d), "snap": i}) for d in (4, 5, 3, 7, 6, 2, 1)]
+
+    def exchange(stage, mine, partners, src_of, dst):
+        for target, dev in partners:
+            remote(src_of(target), dst.at[mine], as_sem.at[stage], ar_sem.at[stage], dev).start()
         pltpu.make_async_copy(src_of(mine), dst.at[mine], ar_sem.at[stage]).start()
         wait_bytes(dst, ar_sem.at[stage])
 
-    exchange(0, 32, q, plane_dev, lambda k: gs.at[k], rx)
+    pl.semaphore_wait(tokens.at[2], 2)
+    exchange(0, q, plane, lambda k: gs.at[k], rx)
     zs[...] = jnp.sum(rx[...], axis=0)
-    exchange(1, 8, z, column_dev, lambda k: zs, rz)
+    exchange(1, z, line, lambda k: zs, rz)
     ag[...] = jnp.sum(rz[...], axis=0)
-    exchange(2, 32, q, plane_dev, lambda k: ag, gf)
+    exchange(2, q, plane, lambda k: ag, gf)
     g_out[...] = gf[...]
 
     for t in range(8):
@@ -318,8 +318,9 @@
             pltpu.VMEM((8, 4, 128), F32),
             pltpu.VMEM((4, 128), F32),
             pltpu.VMEM((32, 4, 128), F32),
-            dma((3,)), dma, dma((10,)), dma((10,)), dma((2, 8)), dma((2, 8)),
+            dma((3,)), dma((4,)), dma((10,)), dma((10,)), dma((2, 8)), dma((2, 8)),
             dma((2,)), dma((2,)), dma((3,)), dma((3,)),
+            pltpu.SemaphoreType.REGULAR((3,)),
         ],
         compiler_params=pltpu.CompilerParams(
             collective_id=0, has_side_effects=True, vmem_limit_bytes=32 << 20

time: 58.8 us -> 56.1 us (0.954)
  Pallas kernels: 58.7 us -> 56 us
    pallas_call x1, Pallas kernels: 54.4 us -> 51.7 us  [gather(): pl.pallas_call(gather_kernel, name='gather', out_shape=(pltpu.VMEM((6, 12...]
where the time goes in v3:
time: 56.1 us; the launch traced here: 56 us
  Pallas kernels  56 us (100%)
    pallas_call x1, Pallas kernels, gather(): pl.pallas_call(gather_kernel, name='gather', out_shape=(pltpu.VMEM((6, 12...  51.7 us
    pallas_call x1, Pallas kernels, whiten(): pl.pallas_call(functools.partial(whiten_kernel, cells), name='whiten', ou...  4.26 us

profile of v3, /device:TPU:1, one launch (start us, length us, event | category | flops | bytes accessed | tf_op | source)
XLA Modules:
  0.0 56.0 jit_solution(1094372961843183872)
XLA Ops:
  0.0 51.7 %gather.1 = (bf16[6,128,1024]{2,1,0:T(8,128)(2,1)S(1)}, bf16[6,128,1024]{2,1,0:T(8,128)(2,1)S(1)}, f32[32,4,128]{2,1,0:T(4,128)S(1)}) custom-call(bf16[16,384,128]{2,1,0:T(8,128)(2,1)} %bitcast.2, bf16[3,2,64,128]{3,2,1,0:T(8,128)(2,1)} %large_hbm.1, f32[64,128]{1,0:T(8,128)} %bitcast.3, f32[4,2,64,128]{3,2,1,0:T(8,128)} %metric_hbm.1), custom_call_target="tpu_custom_call" | custom-call | tf_op jit(solution)/shard_map/gather/pallas_call | solution.py:293
  51.7 4.3 %whiten.1 = f32[128,3,2,8,128]{4,3,2,1,0:T(8,128)} custom-call(bf16[6,128,1024]{2,1,0:T(8,128)(2,1)S(1)} %get-tuple-element.8.vh, bf16[6,128,1024]{2,1,0:T(8,128)(2,1)S(1)} %get-tuple-element.9.vl, f32[32,4,128]{2,1,0:T(4,128)S(1)} %get-tuple-element.10.g_ref), custom_call_target="tpu_custom_call" | custom-call | tf_op jit(solution)/shard_map/whiten/pallas_call | solution.py:382

commit v4 on v3

--- a/solution.py
+++ b/solution.py
@@ -28,7 +28,7 @@
     vh, vl, g_out,
     flow_v, flow_f, send, cols, halo, large_b, large_f, mod_v, mod_b, met,
     acc, gs, rx, zs, rz, ag, gf,
-    in_sem, big_sem, xs_sem, xr_sem, hs_sem, hr_sem, ls_sem, lr_sem, as_sem, ar_sem, tokens,
+    in_sem, big_sem, xs_sem, xr_sem, hs_sem, hr_sem, ls_sem, lr_sem, as_sem, ar_sem, edge_sem, tokens,
 ):
     slab = lax.axis_index("slab")
     i = lax.axis_index("snap")
@@ -50,9 +50,9 @@
 
     flow_in = [
         pltpu.make_async_copy(
-            flow_hbm.at[pl.ds(4 * k, 4)], flow_v.at[pl.ds(4 * k, 4)], big_sem.at[k]
+            flow_hbm.at[:, pl.ds(128 * c, 128)], flow_v.at[:, pl.ds(128 * c, 128)], big_sem.at[c]
         )
-        for k in range(4)
+        for c in range(3)
     ]
     for copy in flow_in:
         copy.start()
@@ -65,60 +65,82 @@
     )
     met_in.start()
 
-    def widen(s, carry):
-        for cy in range(6):
-            for b in range(8):
-                row = pl.multiple_of((cy * 8 + b) * 128 + 8 * s, 8)
-                flow_f[pl.ds(row, 8), :] = flow_v[s, pl.ds(cy * 64 + 8 * b, 8), :].astype(F32)
-        return carry
-
-    for k in range(4):
-        flow_in[k].wait()
-        lax.fori_loop(4 * k, 4 * k + 4, widen, 0)
-
-    def transpose(t):
+    def widen(c):
+        def one(s, carry):
+            for p in range(2):
+                for b in range(8):
+                    cy = 2 * c + p
+                    row = pl.multiple_of((cy * 8 + b) * 128 + 8 * s, 8)
+                    flow_f[pl.ds(row, 8), :] = flow_v[s, pl.ds(cy * 64 + 8 * b, 8), :].astype(F32)
+            return carry
+
+        lax.fori_loop(0, 16, one, 0)
+
+    def transpose(t, c):
         for b in range(8):
-            for cy in range(6):
-                tile = flow_f[pl.ds((cy * 8 + b) * 128 + t, 16, stride=8), :]
-                send[8 * b + t, cy // 2, cy % 2] = tile.astype(BF16)
-
-    transpose(0)
-    pl.semaphore_wait(barrier, len(greeted))
-    for dev in z_side:
-        pl.semaphore_signal(tokens.at[0], inc=1, device_id=dev, device_id_type=MESH)
-
-    mine16 = pl.ds(pl.multiple_of(16 * i, 16), 16)
+            for p in range(2):
+                tile = flow_f[pl.ds(((2 * c + p) * 8 + b) * 128 + t, 16, stride=8), :]
+                send[8 * b + t, c, p] = tile.astype(BF16)
+
+    def block(d):
+        return pl.ds(16 * d, 16)
+
     rows8 = pl.ds(pl.multiple_of(8 * i, 8), 8)
-    def send_step(t, carry):
-        @pl.when(t < 7)
-        def _():
-            transpose(t + 1)
-
+
+    def send_unit(t, c):
+        for side in range(2):
+            remote(
+                send.at[8 * i + t, c, side], halo.at[1 - side, t, c, block(0)],
+                hs_sem.at[side, t], hr_sem.at[1 - side, t], side_dev[side],
+            ).start()
         for d in row_order:
             target = i ^ d
             remote(
-                send.at[8 * target + t], cols.at[t + 1, :, :, mine16, :],
-                xs_sem.at[t + 1], xr_sem.at[t + 1], {"slab": slab, "snap": target},
+                send.at[8 * target + t, c], cols.at[t + 1, c, :, block(d), :],
+                xs_sem.at[t + 1], xr_sem.at[t + 1, c], {"slab": slab, "snap": target},
             ).start()
         pltpu.make_async_copy(
-            send.at[8 * i + t], cols.at[t + 1, :, :, mine16, :], xr_sem.at[t + 1]
+            send.at[8 * i + t, c], cols.at[t + 1, c, :, block(0), :], xr_sem.at[t + 1, c]
         ).start()
+
+    flow_in[0].wait()
+    widen(0)
+    transpose(0, 0)
+    pl.semaphore_wait(barrier, len(greeted))
+    for c in (1, 2):
+        flow_in[c].wait()
+        send_unit(0, c - 1)
+        if c == 1:
+            for dev in z_side:
+                pl.semaphore_signal(tokens.at[0], inc=1, device_id=dev, device_id_type=MESH)
+        widen(c)
+        transpose(0, c)
+
+    def send_step(u, carry):
+        @pl.when(u < 23)
+        def _():
+            transpose(lax.div(u + 1, 3), lax.rem(u + 1, 3))
+
+        send_unit(lax.div(u, 3), lax.rem(u, 3))
         return carry
 
-    lax.fori_loop(0, 8, send_step, 0)
-    for slot, shift in ((0, 63), (9, 8)):
-        for d in row_order:
-            target = i ^ d
-            remote(
-                send.at[lax.rem(8 * target + shift, 64), pl.ds(1, 2)],
-                cols.at[slot, pl.ds(1, 2), :, mine16, :],
-                xs_sem.at[slot], xr_sem.at[slot], {"slab": slab, "snap": target},
-            ).start()
-        pltpu.make_async_copy(
-            send.at[lax.rem(8 * i + shift, 64), pl.ds(1, 2)],
-            cols.at[slot, pl.ds(1, 2), :, mine16, :], xr_sem.at[slot],
+    lax.fori_loop(2, 24, send_step, 0)
+
+    def edge_of(k):
+        core = lax.rem(k, 2)
+        return send.at[lax.rem(8 * k + 63 + 9 * core, 64), pl.ds(1, 2)], 9 * core
+
+    for d in row_order:
+        target = i ^ d
+        source, slot = edge_of(target)
+        remote(
+            source, cols.at[slot, pl.ds(1, 2), :, block(d), :],
+            edge_sem.at[0], xr_sem.at[slot, 0], {"slab": slab, "snap": target},
         ).start()
-
+    source, slot = edge_of(i)
+    pltpu.make_async_copy(
+        source, cols.at[slot, pl.ds(1, 2), :, block(0), :], xr_sem.at[slot, 0]
+    ).start()
     large_in.wait()
     for c in range(3):
         for p in range(2):
@@ -147,19 +169,22 @@
     met_in.wait()
     acc[...] = jnp.zeros((128, 256), F32)
 
-    def pass_on(xx):
-        wait_bytes(cols.at[xx], xr_sem.at[xx])
+    rest = pl.ds(16, 112)
+
+    def pass_on(xx, c):
+        wait_bytes(cols.at[xx, c], xr_sem.at[xx, c])
         for side in range(2):
             remote(
-                cols.at[xx, :, side], halo.at[1 - side, xx - 1],
+                cols.at[xx, c, side, rest], halo.at[1 - side, xx - 1, c, rest],
                 hs_sem.at[side, xx - 1], hr_sem.at[1 - side, xx - 1], side_dev[side],
             ).start()
 
     def pass_step(k, carry):
-        pass_on(k + 1)
+        for c in range(3):
+            pass_on(k + 1, c)
         return carry
 
-    lax.fori_loop(0, 3, pass_step, 0)
+    lax.fori_loop(0, 4, pass_step, 0)
     for copy in large_copies:
         copy.wait()
 
@@ -173,16 +198,20 @@
 
 
     def column(k, carry):
-        xx = lax.rem(k + 1, 8) + 1
-
-        @pl.when(k < 5)
-        def _():
-            pass_on(k + 4)
+        xx = k + 2 - 7 * lax.div(k, 6) + 6 * lax.div(k, 7)
+
+        @pl.when(k < 4)
+        def _():
+            for c in range(3):
+                pass_on(k + 5, c)
 
         @pl.when(k == 6)
         def _():
-            wait_bytes(cols.at[0, pl.ds(1, 2)], xr_sem.at[0])
-            wait_bytes(cols.at[9, pl.ds(1, 2)], xr_sem.at[9])
+            wait_bytes(cols.at[0, pl.ds(1, 2)], xr_sem.at[0, 0])
+
+        @pl.when(k == 7)
+        def _():
+            wait_bytes(cols.at[9, pl.ds(1, 2)], xr_sem.at[9, 0])
 
         for side in range(2):
             wait_bytes(halo.at[side, xx - 1], hr_sem.at[side, xx - 1])
@@ -206,9 +235,10 @@
 
         def snaps(s, inner):
             r = pl.ds(pl.multiple_of(16 * s, 16), 16)
-            m0 = mod_b[xx, r, :]
-            mm = mod_b[xx - 1, r, :]
-            mp = mod_b[xx + 1, r, :]
+            own = pl.ds(pl.multiple_of(16 * (s ^ i), 16), 16)
+            m0 = mod_b[xx, own, :]
+            mm = mod_b[xx - 1, own, :]
+            mp = mod_b[xx + 1, own, :]
 
             def field(c):
                 return [
@@ -239,11 +269,22 @@
                 )
                 for c in range(3):
                     high = around[c].astype(BF16)
-                    vh[2 * c + p, r, lanes] = high
-                    vl[2 * c + p, r, lanes] = (around[c] - high.astype(F32)).astype(BF16)
+                    vh[2 * c + p, own, lanes] = high
+                    vl[2 * c + p, own, lanes] = (around[c] - high.astype(F32)).astype(BF16)
             return inner
 
-        lax.fori_loop(0, 8, snaps, 0, unroll=2)
+        lax.fori_loop(0, 8, snaps, 0, unroll=4)
+
+        @pl.when(k == 3)
+        def _():
+            core = lax.rem(i, 2)
+            for b in range(8):
+                remote(
+                    cols.at[8 - 7 * core, pl.ds(1, 2), :, block(b), :],
+                    cols.at[9 * core, pl.ds(1, 2), :, block(b ^ 1), :],
+                    edge_sem.at[1], xr_sem.at[9 * core, 0], {"slab": slab, "snap": i ^ 1},
+                ).start()
+
         rows_h = jnp.concatenate([vh[cy, :, lanes] for cy in range(6)], axis=1)
         rows_l = jnp.concatenate([vl[cy, :, lanes] for cy in range(6)], axis=1)
         both = jnp.concatenate([rows_h, rows_l], axis=0)
@@ -277,8 +318,8 @@
 
     for t in range(8):
         wait_bytes(send.at[pl.ds(0, 7)], xs_sem.at[t + 1])
-    for slot in (0, 9):
-        wait_bytes(send.at[pl.ds(0, 7), pl.ds(1, 2)], xs_sem.at[slot])
+    wait_bytes(send.at[pl.ds(0, 7), pl.ds(1, 2)], edge_sem.at[0])
+    wait_bytes(cols.at[0, pl.ds(1, 2)], edge_sem.at[1])
     for side in range(2):
         for k in range(8):
             wait_bytes(cols.at[k + 1, :, side], hs_sem.at[side, k])
@@ -318,8 +359,8 @@
             pltpu.VMEM((8, 4, 128), F32),
             pltpu.VMEM((4, 128), F32),
             pltpu.VMEM((32, 4, 128), F32),
-            dma((3,)), dma((4,)), dma((10,)), dma((10,)), dma((2, 8)), dma((2, 8)),
-            dma((2,)), dma((2,)), dma((3,)), dma((3,)),
+            dma((3,)), dma((3,)), dma((10,)), dma((10, 3)), dma((2, 8)), dma((2, 8)),
+            dma((2,)), dma((2,)), dma((3,)), dma((3,)), dma((2,)),
             pltpu.SemaphoreType.REGULAR((3,)),
         ],
         compiler_params=pltpu.CompilerParams(
@@ -356,16 +397,15 @@
         if repeat < NSITER - 1:
             approx = dot(approx, factor)
         inverse = dot(factor, inverse)
-    weights = inverse / jnp.sqrt(frob_scale)
-    w_high = weights.astype(BF16)
-    w_low = (weights - w_high.astype(F32)).astype(BF16)
+    left = jnp.concatenate(
+        [jnp.concatenate([w, w], axis=1) for w in halves(inverse / jnp.sqrt(frob_scale))], axis=0
+    )
 
     stores = []
     for k in range(6):
-        high = vh[k]
-        result = jnp.dot(w_high, high, preferred_element_type=F32)
-        result += jnp.dot(w_high, vl[k], preferred_element_type=F32)
-        result += jnp.dot(w_low, high, preferred_element_type=F32)
+        right = jnp.concatenate([vh[k], vl[k]], axis=0)
+        parts = jnp.dot(left, right, preferred_element_type=F32)
+        result = parts[:128] + parts[128:]
         for x in range(8):
             out_v[k, pl.ds(x, 128, stride=8), :] = result[:, 128 * x : 128 * (x + 1)]
         store = pltpu.make_async_copy(

time: 56.1 us -> 53.2 us (0.948)
  Pallas kernels: 56 us -> 53.1 us
    pallas_call x1, Pallas kernels: 51.7 us -> 49 us  [gather(): pl.pallas_call(gather_kernel, name='gather', out_shape=(pltpu.VMEM((6, 12...]
where the time goes in v4:
time: 53.2 us; the launch traced here: 53.1 us
  Pallas kernels  53.1 us (100%)
    pallas_call x1, Pallas kernels, gather(): pl.pallas_call(gather_kernel, name='gather', out_shape=(pltpu.VMEM((6, 12...  49 us
    pallas_call x1, Pallas kernels, whiten(): pl.pallas_call(functools.partial(whiten_kernel, cells), name='whiten', ou...  4.03 us

profile of v4, /device:TPU:1, one launch (start us, length us, event | category | flops | bytes accessed | tf_op | source)
XLA Modules:
  0.0 53.1 jit_solution(7940699155281964127)
XLA Ops:
  0.0 49.0 %gather.1 = (bf16[6,128,1024]{2,1,0:T(8,128)(2,1)S(1)}, bf16[6,128,1024]{2,1,0:T(8,128)(2,1)S(1)}, f32[32,4,128]{2,1,0:T(4,128)S(1)}) custom-call(bf16[16,384,128]{2,1,0:T(8,128)(2,1)} %bitcast.2, bf16[3,2,64,128]{3,2,1,0:T(8,128)(2,1)} %large_hbm.1, f32[64,128]{1,0:T(8,128)} %bitcast.3, f32[4,2,64,128]{3,2,1,0:T(8,128)} %metric_hbm.1), custom_call_target="tpu_custom_call" | custom-call | tf_op jit(solution)/shard_map/gather/pallas_call | solution.py:334
  49.0 4.0 %whiten.1 = f32[128,3,2,8,128]{4,3,2,1,0:T(8,128)} custom-call(bf16[6,128,1024]{2,1,0:T(8,128)(2,1)S(1)} %get-tuple-element.8.vh, bf16[6,128,1024]{2,1,0:T(8,128)(2,1)S(1)} %get-tuple-element.9.vl, f32[32,4,128]{2,1,0:T(4,128)S(1)} %get-tuple-element.10.g_ref), custom_call_target="tpu_custom_call" | custom-call | tf_op jit(solution)/shard_map/whiten/pallas_call | solution.py:422

commit v5 on v4

--- a/solution.py
+++ b/solution.py
@@ -44,7 +44,8 @@
     row_dev = [{"slab": slab, "snap": i ^ d} for d in row_order]
     y_dev = [{"slab": slab ^ d, "snap": i} for d in (2, 1, 3)]
     barrier = pltpu.get_barrier_semaphore()
-    greeted = row_dev + y_dev + side_dev + z_side
+    cross_dev = [{"slab": down, "snap": i ^ 1}, {"slab": up, "snap": i ^ 1}]
+    greeted = row_dev + y_dev + side_dev + cross_dev + z_side
     for dev in greeted:
         pl.semaphore_signal(barrier, inc=1, device_id=dev, device_id_type=MESH)
 
@@ -88,11 +89,13 @@
     rows8 = pl.ds(pl.multiple_of(8 * i, 8), 8)
 
     def send_unit(t, c):
-        for side in range(2):
-            remote(
-                send.at[8 * i + t, c, side], halo.at[1 - side, t, c, block(0)],
-                hs_sem.at[side, t], hr_sem.at[1 - side, t], side_dev[side],
-            ).start()
+        for e in range(2):
+            for side in range(2):
+                remote(
+                    send.at[8 * (i ^ e) + t, c, side], halo.at[1 - side, t, c, block(e)],
+                    hs_sem.at[side, t], hr_sem.at[1 - side, t],
+                    {"slab": (down, up)[side], "snap": i ^ e},
+                ).start()
         for d in row_order:
             target = i ^ d
             remote(
@@ -169,7 +172,7 @@
     met_in.wait()
     acc[...] = jnp.zeros((128, 256), F32)
 
-    rest = pl.ds(16, 112)
+    rest = pl.ds(32, 96)
 
     def pass_on(xx, c):
         wait_bytes(cols.at[xx, c], xr_sem.at[xx, c])
@@ -184,7 +187,7 @@
             pass_on(k + 1, c)
         return carry
 
-    lax.fori_loop(0, 4, pass_step, 0)
+    lax.fori_loop(0, 3, pass_step, 0)
     for copy in large_copies:
         copy.wait()
 
@@ -200,10 +203,10 @@
     def column(k, carry):
         xx = k + 2 - 7 * lax.div(k, 6) + 6 * lax.div(k, 7)
 
-        @pl.when(k < 4)
+        @pl.when(k < 5)
         def _():
             for c in range(3):
-                pass_on(k + 5, c)
+                pass_on(k + 4, c)
 
         @pl.when(k == 6)
         def _():
@@ -275,7 +278,7 @@
 
         lax.fori_loop(0, 8, snaps, 0, unroll=4)
 
-        @pl.when(k == 3)
+        @pl.when(k == 4)
         def _():
             core = lax.rem(i, 2)
             for b in range(8):
@@ -302,30 +305,29 @@
     plane = [(q ^ d, {"slab": slab ^ (d >> 3), "snap": i ^ (d & 7)}) for d in plane_order]
     line = [(z ^ d, {"slab": slab ^ (4 * d), "snap": i}) for d in (4, 5, 3, 7, 6, 2, 1)]
 
-    def exchange(stage, mine, partners, src_of, dst):
+    def exchange(stage, mine, partners, src_of, dst, drain):
         for target, dev in partners:
             remote(src_of(target), dst.at[mine], as_sem.at[stage], ar_sem.at[stage], dev).start()
         pltpu.make_async_copy(src_of(mine), dst.at[mine], ar_sem.at[stage]).start()
+        drain()
         wait_bytes(dst, ar_sem.at[stage])
 
+    def drain_columns():
+        for t in range(8):
+            wait_bytes(send.at[pl.ds(0, 7)], xs_sem.at[t + 1])
+        wait_bytes(send.at[pl.ds(0, 7), pl.ds(1, 2)], edge_sem.at[0])
+        wait_bytes(cols.at[0, pl.ds(1, 2)], edge_sem.at[1])
+        for side in range(2):
+            for k in range(8):
+                wait_bytes(cols.at[k + 1, :, side], hs_sem.at[side, k])
+
     pl.semaphore_wait(tokens.at[2], 2)
-    exchange(0, q, plane, lambda k: gs.at[k], rx)
+    exchange(0, q, plane, lambda k: gs.at[k], rx, drain_columns)
     zs[...] = jnp.sum(rx[...], axis=0)
-    exchange(1, z, line, lambda k: zs, rz)
+    exchange(1, z, line, lambda k: zs, rz, lambda: wait_bytes(rx.at[pl.ds(0, 31)], as_sem.at[0]))
     ag[...] = jnp.sum(rz[...], axis=0)
-    exchange(2, q, plane, lambda k: ag, gf)
-    g_out[...] = gf[...]
-
-    for t in range(8):
-        wait_bytes(send.at[pl.ds(0, 7)], xs_sem.at[t + 1])
-    wait_bytes(send.at[pl.ds(0, 7), pl.ds(1, 2)], edge_sem.at[0])
-    wait_bytes(cols.at[0, pl.ds(1, 2)], edge_sem.at[1])
-    for side in range(2):
-        for k in range(8):
-            wait_bytes(cols.at[k + 1, :, side], hs_sem.at[side, k])
-    wait_bytes(rx.at[pl.ds(0, 31)], as_sem.at[0])
-    wait_bytes(rz.at[pl.ds(0, 7)], as_sem.at[1])
-    wait_bytes(gf.at[pl.ds(0, 31)], as_sem.at[2])
+    exchange(2, q, plane, lambda k: ag, g_out, lambda: wait_bytes(rz.at[pl.ds(0, 7)], as_sem.at[1]))
+    wait_bytes(g_out.at[pl.ds(0, 31)], as_sem.at[2])
 
 
 def gather(flow, large, mod_t, metric):

time: 53.2 us -> 53.1 us (level)
  no operation moved by 1% of the time
where the time goes in v5:
time: 53.1 us
  Pallas kernels  53 us (100%)
    pallas_call x1, Pallas kernels, gather(): pl.pallas_call(gather_kernel, name='gather', out_shape=(pltpu.VMEM((6, 12...  49 us
    pallas_call x1, Pallas kernels, whiten(): pl.pallas_call(functools.partial(whiten_kernel, cells), name='whiten', ou...  4.03 us

profile of v5, /device:TPU:1, one launch (start us, length us, event | category | flops | bytes accessed | tf_op | source)
XLA Modules:
  0.0 53.1 jit_solution(14640228034112314673)
XLA Ops:
  0.0 49.0 %gather.1 = (bf16[6,128,1024]{2,1,0:T(8,128)(2,1)S(1)}, bf16[6,128,1024]{2,1,0:T(8,128)(2,1)S(1)}, f32[32,4,128]{2,1,0:T(4,128)S(1)}) custom-call(bf16[16,384,128]{2,1,0:T(8,128)(2,1)} %bitcast.2, bf16[3,2,64,128]{3,2,1,0:T(8,128)(2,1)} %large_hbm.1, f32[64,128]{1,0:T(8,128)} %bitcast.3, f32[4,2,64,128]{3,2,1,0:T(8,128)} %metric_hbm.1), custom_call_target="tpu_custom_call" | custom-call | tf_op jit(solution)/shard_map/gather/pallas_call | solution.py:336
  49.0 4.0 %whiten.1 = f32[128,3,2,8,128]{4,3,2,1,0:T(8,128)} custom-call(bf16[6,128,1024]{2,1,0:T(8,128)(2,1)S(1)} %get-tuple-element.8.vh, bf16[6,128,1024]{2,1,0:T(8,128)(2,1)S(1)} %get-tuple-element.9.vl, f32[32,4,128]{2,1,0:T(4,128)S(1)} %get-tuple-element.10.g_ref), custom_call_target="tpu_custom_call" | custom-call | tf_op jit(solution)/shard_map/whiten/pallas_call | solution.py:424

commit v6 on v5

--- a/solution.py
+++ b/solution.py
@@ -116,18 +116,27 @@
         if c == 1:
             for dev in z_side:
                 pl.semaphore_signal(tokens.at[0], inc=1, device_id=dev, device_id_type=MESH)
+            for dev in side_dev:
+                pl.semaphore_signal(tokens.at[3], inc=1, device_id=dev, device_id_type=MESH)
         widen(c)
         transpose(0, c)
 
     def send_step(u, carry):
-        @pl.when(u < 23)
-        def _():
-            transpose(lax.div(u + 1, 3), lax.rem(u + 1, 3))
-
+        transpose(lax.div(u + 1, 3), lax.rem(u + 1, 3))
         send_unit(lax.div(u, 3), lax.rem(u, 3))
         return carry
 
-    lax.fori_loop(2, 24, send_step, 0)
+    lax.fori_loop(2, 23, send_step, 0)
+    send_unit(7, 2)
+    pl.semaphore_wait(tokens.at[3], 2)
+    for side in range(2):
+        for d in row_order[:-1]:
+            target = i ^ d
+            remote(
+                send.at[8 * target + 7, 2, side], halo.at[1 - side, 7, 2, block(d)],
+                hs_sem.at[side, 7], hr_sem.at[1 - side, 7],
+                {"slab": (down, up)[side], "snap": target},
+            ).start()
 
     def edge_of(k):
         core = lax.rem(k, 2)
@@ -176,11 +185,18 @@
 
     def pass_on(xx, c):
         wait_bytes(cols.at[xx, c], xr_sem.at[xx, c])
-        for side in range(2):
-            remote(
-                cols.at[xx, c, side, rest], halo.at[1 - side, xx - 1, c, rest],
-                hs_sem.at[side, xx - 1], hr_sem.at[1 - side, xx - 1], side_dev[side],
-            ).start()
+
+        def forward():
+            for side in range(2):
+                remote(
+                    cols.at[xx, c, side, rest], halo.at[1 - side, xx - 1, c, rest],
+                    hs_sem.at[side, xx - 1], hr_sem.at[1 - side, xx - 1], side_dev[side],
+                ).start()
+
+        if c < 2:
+            forward()
+        else:
+            pl.when(xx < 8)(forward)
 
     def pass_step(k, carry):
         for c in range(3):
@@ -363,7 +379,7 @@
             pltpu.VMEM((32, 4, 128), F32),
             dma((3,)), dma((3,)), dma((10,)), dma((10, 3)), dma((2, 8)), dma((2, 8)),
             dma((2,)), dma((2,)), dma((3,)), dma((3,)), dma((2,)),
-            pltpu.SemaphoreType.REGULAR((3,)),
+            pltpu.SemaphoreType.REGULAR((4,)),
         ],
         compiler_params=pltpu.CompilerParams(
             collective_id=0, has_side_effects=True, vmem_limit_bytes=32 << 20

time: 53.1 us -> 53 us (level)
  no operation moved by 1% of the time
where the time goes in v6:
time: 53 us; the launch traced here: 52.9 us
  Pallas kernels  52.9 us (100%)
    pallas_call x1, Pallas kernels, gather(): pl.pallas_call(gather_kernel, name='gather', out_shape=(pltpu.VMEM((6, 12...  48.9 us
    pallas_call x1, Pallas kernels, whiten(): pl.pallas_call(functools.partial(whiten_kernel, cells), name='whiten', ou...  4.03 us

profile of v6, /device:TPU:1, one launch (start us, length us, event | category | flops | bytes accessed | tf_op | source)
XLA Modules:
  0.0 52.9 jit_solution(7897163468275510941)
XLA Ops:
  0.0 48.9 %gather.1 = (bf16[6,128,1024]{2,1,0:T(8,128)(2,1)S(1)}, bf16[6,128,1024]{2,1,0:T(8,128)(2,1)S(1)}, f32[32,4,128]{2,1,0:T(4,128)S(1)}) custom-call(bf16[16,384,128]{2,1,0:T(8,128)(2,1)} %bitcast.2, bf16[3,2,64,128]{3,2,1,0:T(8,128)(2,1)} %large_hbm.1, f32[64,128]{1,0:T(8,128)} %bitcast.3, f32[4,2,64,128]{3,2,1,0:T(8,128)} %metric_hbm.1), custom_call_target="tpu_custom_call" | custom-call | tf_op jit(solution)/shard_map/gather/pallas_call | solution.py:352
  48.9 4.0 %whiten.1 = f32[128,3,2,8,128]{4,3,2,1,0:T(8,128)} custom-call(bf16[6,128,1024]{2,1,0:T(8,128)(2,1)S(1)} %get-tuple-element.8.vh, bf16[6,128,1024]{2,1,0:T(8,128)(2,1)S(1)} %get-tuple-element.9.vl, f32[32,4,128]{2,1,0:T(4,128)S(1)} %get-tuple-element.10.g_ref), custom_call_target="tpu_custom_call" | custom-call | tf_op jit(solution)/shard_map/whiten/pallas_call | solution.py:440

commit v7 on v6

--- a/solution.py
+++ b/solution.py
@@ -203,7 +203,7 @@
             pass_on(k + 1, c)
         return carry
 
-    lax.fori_loop(0, 3, pass_step, 0)
+    lax.fori_loop(0, 4, pass_step, 0)
     for copy in large_copies:
         copy.wait()
 
@@ -219,10 +219,10 @@
     def column(k, carry):
         xx = k + 2 - 7 * lax.div(k, 6) + 6 * lax.div(k, 7)
 
-        @pl.when(k < 5)
+        @pl.when(k < 4)
         def _():
             for c in range(3):
-                pass_on(k + 4, c)
+                pass_on(k + 5, c)
 
         @pl.when(k == 6)
         def _():
@@ -294,7 +294,7 @@
 
         lax.fori_loop(0, 8, snaps, 0, unroll=4)
 
-        @pl.when(k == 4)
+        @pl.when(k == 3)
         def _():
             core = lax.rem(i, 2)
             for b in range(8):

time: 53 us -> 53 us (level)
  no operation moved by 1% of the time
where the time goes in v7:
time: 53 us; the launch traced here: 52.9 us
  Pallas kernels  52.9 us (100%)
    pallas_call x1, Pallas kernels, gather(): pl.pallas_call(gather_kernel, name='gather', out_shape=(pltpu.VMEM((6, 12...  48.9 us
    pallas_call x1, Pallas kernels, whiten(): pl.pallas_call(functools.partial(whiten_kernel, cells), name='whiten', ou...  4.03 us

profile of v7, /device:TPU:1, one launch (start us, length us, event | category | flops | bytes accessed | tf_op | source)
XLA Modules:
  0.0 52.9 jit_solution(11540301979635331599)
XLA Ops:
  0.0 48.9 %gather.1 = (bf16[6,128,1024]{2,1,0:T(8,128)(2,1)S(1)}, bf16[6,128,1024]{2,1,0:T(8,128)(2,1)S(1)}, f32[32,4,128]{2,1,0:T(4,128)S(1)}) custom-call(bf16[16,384,128]{2,1,0:T(8,128)(2,1)} %bitcast.2, bf16[3,2,64,128]{3,2,1,0:T(8,128)(2,1)} %large_hbm.1, f32[64,128]{1,0:T(8,128)} %bitcast.3, f32[4,2,64,128]{3,2,1,0:T(8,128)} %metric_hbm.1), custom_call_target="tpu_custom_call" | custom-call | tf_op jit(solution)/shard_map/gather/pallas_call | solution.py:352
  48.9 4.0 %whiten.1 = f32[128,3,2,8,128]{4,3,2,1,0:T(8,128)} custom-call(bf16[6,128,1024]{2,1,0:T(8,128)(2,1)S(1)} %get-tuple-element.8.vh, bf16[6,128,1024]{2,1,0:T(8,128)(2,1)S(1)} %get-tuple-element.9.vl, f32[32,4,128]{2,1,0:T(4,128)S(1)} %get-tuple-element.10.g_ref), custom_call_target="tpu_custom_call" | custom-call | tf_op jit(solution)/shard_map/whiten/pallas_call | solution.py:440
